TPU v7x, 32 devices: a whole 2x2x4 slice. The times are simulated.
32 devices in a mesh: expert: 16 (over z, y, x), shard: 2 (over core).
Axes of the slice: x: 2, y: 2, z: 4, core: 2. Of those that a mesh axis runs over, the one named last changes fastest.
Arguments:
- expert_rows: bfloat16 [16, 1536, 5120], P('expert', None, 'shard'), may hold values from -45 to 45
- sketch: bfloat16 [5120, 256], P('shard'), may hold values from -0.078125 to 0.078125
- permutation: int32 [16, 1536], P('expert'), may hold values from 0 to 1535, each once within a row
- clusters: int32 [16], replicated, may hold values from 0 to 3, as said below
- frequency: int32 [16], replicated, may hold values from 20 to 64
Outputs:
- merged: bfloat16 [16, 1536, 1280], P('expert', None, 'shard')
- basis: float32 [16, 384, 256], P('expert', 'shard')
- coefficients: float32 [16, 256, 1280], P('expert', None, 'shard')
Inputs may be any that keep to these rules, and one draw needn't show every extreme that they name: `clusters`: the source experts of merged experts 2 w and 2 w + 1 are exactly the source experts 2 * 4 * w to 2 * 4 * w + 2 * 4 - 1; each merged expert holds 2 to 6 source experts, and some merged expert holds exactly 6.
All inputs are finite; a program needn't handle non-finite values.
Results may differ from a plain program's by a relative error of at most 0.0065.
Values may be sent and summed in bfloat16 or wider, within the bound.
A program may use at most 128 MiB of HBM per device.

v0:
```python
import math

import jax
import jax.numpy as jnp
from jax import lax
from jax.sharding import PartitionSpec as P

FF = 1536
GROUP = 4


def from_partner(value, axis, distance):
    return lax.ppermute(value, axis, [(i, i ^ 1 << distance) for i in range(lax.axis_size(axis))])


def cluster_tables(clusters, frequency):
    expert_count = clusters.shape[0]
    cluster_count = expert_count // GROUP
    membership = clusters[None, :] == jnp.arange(cluster_count, dtype=jnp.int32)[:, None]
    freq_real = frequency.astype(jnp.float32)
    cluster_totals = jnp.sum(jnp.where(membership, freq_real[None, :], jnp.float32(0.0)), axis=1)
    own_total = jnp.sum(jnp.where(membership, cluster_totals[:, None], jnp.float32(0.0)), axis=0)
    merge_weight = (freq_real / own_total).astype(jnp.bfloat16)
    mixing = jnp.where(membership, merge_weight[None, :], jnp.zeros((), jnp.bfloat16))
    return mixing


def on_device(expert_rows, sketch, permutation, clusters, frequency):
    experts = lax.axis_size("expert")
    shard_count = lax.axis_size("shard")
    local_rows = expert_rows[0]
    ff_rows, part_cols = local_rows.shape
    block_cols = part_cols // GROUP
    piece_rows = ff_rows // experts
    position = lax.axis_index("expert")
    own_slot = position % GROUP
    inverse = (
        jnp.zeros((ff_rows,), jnp.int32)
        .at[permutation[0]]
        .set(jnp.arange(ff_rows, dtype=jnp.int32))
    )
    permuted = local_rows[inverse]
    mixing = cluster_tables(clusters, frequency)
    spread = lax.all_to_all(
        permuted.reshape(experts, piece_rows, part_cols),
        "expert",
        split_axis=0,
        concat_axis=0,
        tiled=True,
    )
    spread = spread.reshape(experts, piece_rows, GROUP, block_cols)
    merged_relay = jnp.einsum(
        "ce,etgw->cgtw", mixing, spread, preferred_element_type=jnp.float32
    ).astype(jnp.bfloat16)
    arrived = lax.all_to_all(
        merged_relay.reshape(experts, piece_rows, block_cols),
        "expert",
        split_axis=0,
        concat_axis=0,
        tiled=True,
    )
    merged_block = arrived.reshape(ff_rows, block_cols)
    local_sketch = lax.dynamic_slice_in_dim(sketch, own_slot * block_cols, block_cols, 0)
    partial_sketch = jnp.dot(merged_block, local_sketch, preferred_element_type=jnp.float32)
    for bit_index in range(GROUP.bit_length() - 1):
        partial_sketch = partial_sketch + from_partner(partial_sketch, "expert", bit_index)
    sketched = lax.psum(partial_sketch, "shard")
    gram_matrix = jnp.dot(sketched.T, sketched, precision=lax.Precision.HIGHEST) / FF
    cholesky_factor = jnp.linalg.cholesky(gram_matrix)
    orth = jax.scipy.linalg.solve_triangular(cholesky_factor, sketched.T, lower=True).T
    inv_root = 1.0 / math.sqrt(FF)
    coef_block = (
        jnp.dot(orth.astype(jnp.bfloat16).T, merged_block, preferred_element_type=jnp.float32)
        * inv_root
    )
    basis_rows = ff_rows // (GROUP * shard_count)
    basis_start = (own_slot * shard_count + lax.axis_index("shard")) * basis_rows
    basis_part = lax.dynamic_slice_in_dim(orth, basis_start, basis_rows, 0)
    return (merged_block[None], basis_part[None], coef_block[None])


def solution(mesh):
    return jax.shard_map(
        on_device,
        mesh=mesh,
        in_specs=(P("expert", None, "shard"), P("shard", None), P("expert", None), P(), P()),
        out_specs=(
            P("expert", None, "shard"),
            P("expert", "shard", None),
            P("expert", None, "shard"),
        ),
        check_vma=False,
    )
```

profile of v0, /device:TPU:0, one launch (start us, length us, event | category | flops | bytes accessed | tf_op | source)
XLA Modules:
  0.0 480.2 jit_solution(1204002792275449585)
XLA Ops:
  8.0 6.2 %scatter_custom_fusion = s32[1536]{0:T(1024)S(1)} fusion(s32[1536]{0:T(1024)S(1)} %fusion.20, s32[1536]{0:T(1024)S(1)} %iota.53, s32[]{:T(128)} %copy.33), kind=kCustom, calls=%fused_computation.43 | custom fusion | bytes 6148 | tf_op jit(solution)/shard_map/scatter | solution.py:40
  14.2 19.3 %gather_fusion = bf16[1536,2560]{1,0:T(8,128)(2,1)} fusion(bf16[1536,2560]{1,0:T(8,128)(2,1)} %bitcast.55, s32[2048]{0:T(1024)S(1)} %pad_clamp_fusion), kind=kCustom, calls=%fused_computation | custom fusion | bytes 15734784 | tf_op jit(solution)/shard_map/gather | solution.py:42
  33.6 8.5 %all-to-all-start = ((bf16[16,96,2560]{2,1,0:T(8,128)(2,1)}), bf16[16,96,2560]{2,1,0:T(8,128)(2,1)}, u32[]{:S(2)}, u32[]{:S(2)}) async-start(bf16[16,96,2560]{2,1,0:T(8,128)(2,1)} %bitcast.59), calls=%async_computation | async-start | bytes 15728640 | tf_op jit(solution)/shard_map/all_to_all | solution.py:44
  42.3 148.3 %all-to-all-done = bf16[16,96,2560]{2,1,0:T(8,128)(2,1)} async-done(((bf16[16,96,2560]{2,1,0:T(8,128)(2,1)}), bf16[16,96,2560]{2,1,0:T(8,128)(2,1)}, u32[]{:S(2)}, u32[]{:S(2)}) %all-to-all-start) | async-done | bytes 7864352 | tf_op jit(solution)/shard_map/all_to_all | solution.py:44
  190.6 14.4 %reshape.70 = bf16[16,96,4,640]{3,2,1,0:T(4,128)(2,1)} reshape(bf16[16,96,2560]{2,1,0:T(8,128)(2,1)} %all-to-all-done) | data formatting | bytes 15728640 | tf_op jit(solution)/shard_map/reshape | solution.py:51
  205.0 8.0 %convert_bitcast_fusion = bf16[4,4,96,640]{3,0,1,2:T(4,128)(2,1)S(1)} fusion(bf16[16,96,4,640]{3,2,1,0:T(4,128)(2,1)} %reshape.70, s32[16]{0:T(128)S(1)} %copy-done.7, bf16[16]{0:T(256)(128)(2,1)S(1)} %divide_convert_fusion), kind=kOutput, calls=%fused_computation.6 | convolution fusion | flops 32440448 | bytes 9830496 | tf_op jit(solution)/shard_map/ce,etgw->cgtw/dot_general | solution.py:52
  212.9 1.7 copy.12
  214.6 35.6 %all-to-all-start.1 = ((bf16[16,96,640]{2,1,0:T(8,128)(2,1)}), bf16[16,96,640]{2,1,0:T(8,128)(2,1)S(1)}, u32[]{:S(2)}, u32[]{:S(2)}) async-start(bf16[16,96,640]{2,1,0:T(8,128)(2,1)} %bitcast.62), calls=%async_computation.1 | async-start | bytes 3932160 | tf_op jit(solution)/shard_map/all_to_all | solution.py:55
  250.5 39.7 %all-to-all-done.1 = bf16[16,96,640]{2,1,0:T(8,128)(2,1)S(1)} async-done(((bf16[16,96,640]{2,1,0:T(8,128)(2,1)}), bf16[16,96,640]{2,1,0:T(8,128)(2,1)S(1)}, u32[]{:S(2)}, u32[]{:S(2)}) %all-to-all-start.1) | async-done | bytes 1966112 | tf_op jit(solution)/shard_map/all_to_all | solution.py:55
  291.0 1.0 collective-permute-start
  292.0 33.3 %collective-permute-done = f32[1536,256]{1,0:T(8,128)S(1)} collective-permute-done((f32[1536,256]{1,0:T(8,128)S(1)}, f32[1536,256]{1,0:T(8,128)S(1)}, u32[]{:S(2)}, u32[]{:S(2)}) %collective-permute-start) | collective-permute-done | bytes 1572896 | tf_op jit(solution)/shard_map/ppermute | solution.py:13
  325.4 3.3 collective-permute-start.1
  328.7 31.6 %collective-permute-done.1 = f32[1536,256]{1,0:T(8,128)S(1)} collective-permute-done((f32[1536,256]{1,0:T(8,128)S(1)}, f32[1536,256]{1,0:T(8,128)S(1)}, u32[]{:S(2)}, u32[]{:S(2)}) %collective-permute-start.1) | collective-permute-done | bytes 1572896 | tf_op jit(solution)/shard_map/ppermute | solution.py:13
  360.4 1.3 add.62
  361.8 24.7 %all-reduce.3.cloned.1.call-done = f32[1536,256]{1,0:T(8,128)} async-done(((f32[1536,256]{1,0:T(8,128)}), f32[1536,256]{1,0:T(8,128)}) %all-reduce.3.cloned.1.call-update) | async-done | bytes 1572880 | tf_op jit(solution)/shard_map/psum | solution.py:67
  386.5 4.5 convolution_multiply_fusion.1
  391.9 1.0 fusion.14
  393.6 11.7 %cholesky.50 = f32[128,128]{1,0:T(8,128)S(1)} custom-call(f32[128,128]{1,0:T(8,128)S(1)} %cholesky.118), custom_call_target="Cholesky" | custom-call | tf_op jit(solution)/shard_map/jit(cholesky)/cholesky | solution.py:69
  407.4 11.3 %custom-call.15 = f32[1,128,128]{1,2,0:T(8,128)} custom-call(f32[1,128,128]{2,1,0:T(8,128)} %get-tuple-element.30), custom_call_target="InvertDiagBlocksLowerTriangular" | custom-call | tf_op jit(solution)/shard_map/jit(cholesky)/cholesky | solution.py:69
  418.7 1.1 constant_dynamic-update-slice_fusion
  419.8 1.7 convolution_subtract_fusion
  421.5 13.4 %cholesky.105 = f32[128,128]{1,0:T(8,128)} custom-call(f32[128,128]{1,0:T(8,128)} %convolution_subtract_fusion), custom_call_target="Cholesky" | custom-call | tf_op jit(solution)/shard_map/jit(cholesky)/cholesky | solution.py:69
  434.9 0.9 select_reduce_fusion
  437.7 1.0 select_select_fusion
  438.8 5.2 %while.1 = (s32[]{:T(128)}, f32[256,256]{1,0:T(8,128)S(1)}, s32[2,2]{1,0:T(2,128)S(1)}, f32[2,128,128]{2,1,0:T(8,128)}, s32[]{:T(128)}) while((s32[]{:T(128)}, f32[256,256]{1,0:T(8,128)S(1)}, s32[2,2]{1,0:T(2,128)S(1)}, f32[2,128,128]{2,1,0:T(8,128)}, s32[]{:T(128)}) %tuple.29), condition=%wide.while_cond, body=%wide.while_body.sunk | while | flops 2 | bytes 132205 | solution.py:70
  439.4 2.0 bitcast_dynamic-update-slice_fusion.2
  442.0 2.0 bitcast_dynamic-update-slice_fusion.2
  444.0 21.1 %custom-call.16 = f32[2,128,128]{1,2,0:T(8,128)} custom-call(f32[2,128,128]{2,1,0:T(8,128)} %get-tuple-element.10), custom_call_target="InvertDiagBlocksLowerTriangular" | custom-call | tf_op jit(solution)/shard_map/jit(_solve_triangular)/triangular_solve | solution.py:70
  465.1 2.1 fusion.8
  467.3 1.4 fusion.15
  469.5 1.6 fusion.5
  472.1 1.3 copy.34
  (43 shorter events, 9.7 us)
Async XLA Ops:
  7.2 283.0 %copy-start = (bf16[2560,256]{1,0:T(8,128)(2,1)S(1)}, bf16[2560,256]{1,0:T(8,128)(2,1)}, u32[]{:S(2)}) copy-start(bf16[2560,256]{1,0:T(8,128)(2,1)} %param.6) | copy-start | bytes 3932164
  33.6 8.5 %copy-start.6 = (s32[16]{0:T(128)S(1)}, s32[16]{0:T(128)}, u32[]{:S(2)}) copy-start(s32[16]{0:T(128)} %param.9) | copy-start | bytes 196
  33.6 8.5 %copy-start.7 = (s32[16]{0:T(128)S(1)}, s32[16]{0:T(128)}, u32[]{:S(2)}) copy-start(s32[16]{0:T(128)} %param.8) | copy-start | bytes 196
  33.6 157.0 %all-to-all-start = ((bf16[16,96,2560]{2,1,0:T(8,128)(2,1)}), bf16[16,96,2560]{2,1,0:T(8,128)(2,1)}, u32[]{:S(2)}, u32[]{:S(2)}) async-start(bf16[16,96,2560]{2,1,0:T(8,128)(2,1)} %bitcast.59), calls=%async_computation | async-start | bytes 15728640 | tf_op jit(solution)/shard_map/all_to_all | solution.py:44
  214.6 75.6 %all-to-all-start.1 = ((bf16[16,96,640]{2,1,0:T(8,128)(2,1)}), bf16[16,96,640]{2,1,0:T(8,128)(2,1)S(1)}, u32[]{:S(2)}, u32[]{:S(2)}) async-start(bf16[16,96,640]{2,1,0:T(8,128)(2,1)} %bitcast.62), calls=%async_computation.1 | async-start | bytes 3932160 | tf_op jit(solution)/shard_map/all_to_all | solution.py:55
  250.2 136.2 %all-reduce.3.cloned.1.call-start = ((), (), s32[]{:S(2)}) async-start(), calls=%async_computation.2 | async-start | bytes 3145728 | tf_op jit(solution)/shard_map/psum | solution.py:67
  291.0 34.3 %collective-permute-start = (f32[1536,256]{1,0:T(8,128)S(1)}, f32[1536,256]{1,0:T(8,128)S(1)}, u32[]{:S(2)}, u32[]{:S(2)}) collective-permute-start(f32[1536,256]{1,0:T(8,128)S(1)} %fusion.10), channel_id=1, source_target_pairs={{0,2},{2,0},{4,6},{6,4},{8,10},{10,8},{12,14},{14,12},{16,18},{18,... | collective-permute-start | bytes 4718600 | tf_op jit(solution)/shard_map/ppermute | solution.py:13
  325.4 34.9 %collective-permute-start.1 = (f32[1536,256]{1,0:T(8,128)S(1)}, f32[1536,256]{1,0:T(8,128)S(1)}, u32[]{:S(2)}, u32[]{:S(2)}) collective-permute-start(f32[1536,256]{1,0:T(8,128)S(1)} %add.61), channel_id=1, source_target_pairs={{0,4},{2,6},{4,0},{6,2},{8,12},{10,14},{12,8},{14,10},{16,20},{18,... | collective-permute-start | bytes 4718600 | tf_op jit(solution)/shard_map/ppermute | solution.py:13
  392.9 0.7 copy-start.3
  405.3 0.6 copy-start.4
  435.8 1.9 copy-start.2
  465.1 3.6 copy-start.1
  465.1 3.6 copy-start.5
Sparse Core Ops, SparseCore 0:
  361.9 24.5 all-reduce.2
where the time goes:
time: 481 us; the launch traced here: 480 us
  waiting for transfers between devices  278 us (58%)
  other arithmetic  64.4 us (13%)
  local copies, waits for them, and re-layouts  52 us (11%)
  starting transfers between devices  48.7 us (10%)
  matrix products  22.1 us (5%)
  between operations  15.5 us (3%)
    all_to_all x1, waiting for transfers between devices, on_device(): lax.all_to_all(permuted.reshape(experts, piece_rows, part_cols), 'expert'...  148 us
    ppermute x2, waiting for transfers between devices, from_partner(): lax.ppermute(value, axis, [(i, i ^ 1 << distance) for i in range(lax.axis...  64.9 us
    all_to_all x1, waiting for transfers between devices, on_device(): lax.all_to_all(merged_relay.reshape(experts, piece_rows, block_cols), 'ex...  39.7 us
    another operation x6, other arithmetic, on_device(): cholesky_factor = jnp.linalg.cholesky(gram_matrix)  38.6 us
    all_to_all x1, starting transfers between devices, on_device(): lax.all_to_all(merged_relay.reshape(experts, piece_rows, block_cols), 'ex...  35.6 us
    psum x1, waiting for transfers between devices, on_device(): sketched = lax.psum(partial_sketch, 'shard')  24.7 us
    another operation x3, other arithmetic, on_device(): jax.scipy.linalg.solve_triangular(cholesky_factor, sketched.T, lower=True)  22.1 us
    gather x1, local copies, waits for them, and re-layouts, on_device(): permuted = local_rows[inverse]  19.3 us
  transfers between devices with their start and end apart: 5, of which 5 were waited for; matrix products, arithmetic and copies ran while one was open for 0% of the time, Pallas kernels for 0%

commit v1 on v0

v1 whole, which is shorter than its diff:
```python
import math

import jax
import jax.numpy as jnp
from jax import lax
from jax.experimental import pallas as pl
from jax.experimental.pallas import tpu as pltpu
from jax.sharding import PartitionSpec as P

GROUP = 4
MESH = pl.DeviceIdType.MESH
LIMIT = 60 * 1024 * 1024


def column_chunks(width):
    chunks, start = [], 0
    while start < width:
        step = min(256, width - start)
        chunks.append((start, step))
        start += step
    return chunks


def merge_kernel(
    mix_ref,
    perm_ref,
    rows_ref,
    sketch_ref,
    merged_ref,
    full_ref,
    peer_perm,
    onehot,
    blocks,
    kept,
    zsend,
    zrecv,
    sk,
    part,
    core_rx,
    summed,
    group_rx,
    mine,
    gathered,
    perm_send,
    perm_recv,
    own_sem,
    sk_sem,
    row_send,
    row_recv,
    z_send,
    z_recv,
    core_send,
    core_recv,
    rs_send,
    rs_recv,
    ag_send,
    ag_recv,
    fw_send,
    fw_recv,
):
    position = lax.axis_index("expert")
    core = lax.axis_index("shard")
    slot = lax.rem(position, GROUP)
    plane = position - slot
    other_core = 1 - core
    ff, width = merged_ref.shape
    tile = ff // GROUP
    half = tile // 2
    rank = full_ref.shape[1]
    chunks = column_chunks(width)
    peer_slot = {
        0: slot,
        1: slot + 1 - 2 * lax.rem(slot, 2),
        2: slot + 2 - 4 * lax.div(slot, 2),
        3: 3 - slot,
    }
    peer = {d: {"expert": plane + peer_slot[d]} for d in (1, 2, 3)}
    across = {"expert": position + 4 - 8 * lax.rem(lax.div(position, 4), 2)}
    beside = {"shard": other_core}

    barrier = pltpu.get_barrier_semaphore()
    for target in (peer[1], peer[2], peer[3], across, beside):
        pl.semaphore_signal(barrier, inc=1, device_id=target, device_id_type=MESH)

    own_copy = pltpu.make_async_copy(
        rows_ref.at[:, pl.ds(pl.multiple_of(slot * width, 128), width)], blocks.at[0], own_sem
    )
    own_copy.start()
    sk_copy = pltpu.make_async_copy(
        sketch_ref.at[pl.ds(pl.multiple_of(slot * width, 128), width), :], sk, sk_sem
    )
    sk_copy.start()
    pl.semaphore_wait(barrier, 5)

    def remote(src, dst, send, recv, target):
        return pltpu.make_async_remote_copy(
            src_ref=src,
            dst_ref=dst,
            send_sem=send,
            recv_sem=recv,
            device_id=target,
            device_id_type=MESH,
        )

    perm_copies = {
        d: remote(perm_ref, peer_perm.at[d - 1], perm_send.at[d - 1], perm_recv.at[d - 1], peer[d])
        for d in (3, 1, 2)
    }
    for copy in perm_copies.values():
        copy.start()
    row_copies = {}
    for c, (start, step) in enumerate(chunks):
        for d in (3, 1, 2):
            first = pl.multiple_of(peer_slot[d] * width + start, 128)
            row_copies[c, d] = remote(
                rows_ref.at[:, pl.ds(first, step)],
                blocks.at[d, :, pl.ds(start, step)],
                row_send.at[c, d - 1],
                row_recv.at[c, d - 1],
                peer[d],
            )
            row_copies[c, d].start()

    def build(d, values):
        @pl.loop(0, 2 * GROUP)
        def _(t):
            first = pl.multiple_of(t * half, half)
            index = lax.broadcasted_iota(jnp.int32, (half, ff), 0) + first
            onehot[d, pl.ds(first, half), :] = jnp.where(index == values, 1.0, 0.0).astype(
                jnp.bfloat16
            )

    build(0, perm_ref[...])
    for d in (1, 2, 3):
        perm_copies[d].wait()
        build(d, peer_perm[d - 1])
    own_copy.wait()
    sk_copy.wait()

    def z_copy(c, t):
        start, step = chunks[c]
        first = pl.multiple_of(t * tile, tile)
        view = (pl.ds(first, tile), pl.ds(start, step))
        return remote(zsend.at[view], zrecv.at[view], z_send.at[c, t], z_recv.at[c, t], across)

    def compute(c):
        start, step = chunks[c]
        for d in (1, 2, 3):
            row_copies[c, d].wait()

        @pl.loop(0, GROUP)
        def _(t):
            first = pl.multiple_of(t * tile, tile)
            keep = jnp.zeros((tile, step), jnp.float32)
            give = jnp.zeros((tile, step), jnp.float32)
            for d in range(4):
                moved = jnp.dot(
                    onehot[d, pl.ds(first, tile), :],
                    blocks[d, :, start : start + step],
                    preferred_element_type=jnp.float32,
                )
                keep = keep + mix_ref[0, d] * moved
                give = give + mix_ref[1, d] * moved
            kept[pl.ds(first, tile), start : start + step] = keep
            zsend[pl.ds(first, tile), start : start + step] = give.astype(jnp.bfloat16)
            z_copy(c, t).start()

    def finalize(c, t):
        start, step = chunks[c]
        first = pl.multiple_of(t * tile, tile)
        z_copy(c, t).wait()
        merged_ref[pl.ds(first, tile), start : start + step] = (
            kept[pl.ds(first, tile), start : start + step]
            + zrecv[pl.ds(first, tile), start : start + step].astype(jnp.float32)
        ).astype(jnp.bfloat16)

    last = len(chunks) - 1
    for c in range(last + 1):
        compute(c)
        if c >= 1:

            @pl.loop(0, GROUP)
            def _(t):
                finalize(c - 1, t)

    def core_copy(t):
        first = pl.multiple_of(t * tile + other_core * half, half)
        return remote(
            part.at[pl.ds(first, half), :],
            core_rx.at[t],
            core_send.at[t],
            core_recv.at[t],
            beside,
        )

    @pl.loop(0, GROUP)
    def _(t):
        finalize(last, t)
        first = pl.multiple_of(t * tile, tile)
        part[pl.ds(first, tile), :] = jnp.dot(
            merged_ref[pl.ds(first, tile), :], sk[...], preferred_element_type=jnp.float32
        )
        core_copy(t).start()

    @pl.loop(0, GROUP)
    def _(t):
        core_copy(t).wait()
        first = pl.multiple_of(t * tile + core * half, half)
        summed[t] = part[pl.ds(first, half), :] + core_rx[t]

    rs_copies = {}
    for d in (3, 1, 2):
        rs_copies[d] = remote(
            summed.at[peer_slot[d]],
            group_rx.at[d - 1],
            rs_send.at[d - 1],
            rs_recv.at[d - 1],
            peer[d],
        )
        rs_copies[d].start()
    total = summed[slot]
    for d in (1, 2, 3):
        rs_copies[d].wait()
        total = total + group_rx[d - 1]
    mine[...] = total
    place = slot * 2 + core
    ag_copies = {}
    for d in (3, 1, 2):
        ag_copies[d] = remote(
            mine, gathered.at[place], ag_send.at[d - 1], ag_recv.at[d - 1], peer[d]
        )
        ag_copies[d].start()
    forwards = [remote(mine, gathered.at[place], fw_send.at[0], fw_recv.at[0], beside)]
    forwards[0].start()
    gathered[place] = total
    for d in (1, 2, 3):
        ag_copies[d].wait()
        came = peer_slot[d] * 2 + core
        forwards.append(
            remote(gathered.at[came], gathered.at[came], fw_send.at[d], fw_recv.at[d], beside)
        )
        forwards[d].start()
    for copy in forwards:
        copy.wait()
    for b in range(2 * GROUP):
        full_ref[b * half : (b + 1) * half, :] = gathered[b]


def merge(mix, perm, rows, sketch):
    ff, part_cols = rows.shape
    width = part_cols // GROUP
    rank = sketch.shape[1]
    half = ff // (2 * GROUP)
    chunks = len(column_chunks(width))
    dma = pltpu.SemaphoreType.DMA
    vmem = pl.BlockSpec(memory_space=pltpu.VMEM)
    f32, bf16 = jnp.float32, jnp.bfloat16
    return pl.pallas_call(
        merge_kernel,
        out_shape=(
            jax.ShapeDtypeStruct((ff, width), bf16),
            jax.ShapeDtypeStruct((ff, rank), f32),
        ),
        in_specs=[
            pl.BlockSpec(memory_space=pltpu.SMEM),
            vmem,
            pl.BlockSpec(memory_space=pl.ANY),
            pl.BlockSpec(memory_space=pl.ANY),
        ],
        out_specs=(vmem, vmem),
        scratch_shapes=[
            pltpu.VMEM((3, 1, ff), jnp.int32),
            pltpu.VMEM((4, ff, ff), bf16),
            pltpu.VMEM((4, ff, width), bf16),
            pltpu.VMEM((ff, width), f32),
            pltpu.VMEM((ff, width), bf16),
            pltpu.VMEM((ff, width), bf16),
            pltpu.VMEM((width, rank), bf16),
            pltpu.VMEM((ff, rank), f32),
            pltpu.VMEM((GROUP, half, rank), f32),
            pltpu.VMEM((GROUP, half, rank), f32),
            pltpu.VMEM((3, half, rank), f32),
            pltpu.VMEM((half, rank), f32),
            pltpu.VMEM((2 * GROUP, half, rank), f32),
            dma((3,)),
            dma((3,)),
            dma,
            dma,
            dma((chunks, 3)),
            dma((chunks, 3)),
            dma((chunks, GROUP)),
            dma((chunks, GROUP)),
            dma((GROUP,)),
            dma((GROUP,)),
            dma((3,)),
            dma((3,)),
            dma((3,)),
            dma((3,)),
            dma((4,)),
            dma((4,)),
        ],
        compiler_params=pltpu.CompilerParams(
            collective_id=0, has_side_effects=True, vmem_limit_bytes=LIMIT
        ),
        name="merge",
    )(mix, perm, rows, sketch)


def exact_dot(left, right, dims):
    return lax.dot_general(
        left,
        right,
        (dims, ((), ())),
        precision=lax.Precision.HIGHEST,
        preferred_element_type=jnp.float32,
    )


def inverse_factor(matrix):
    size = matrix.shape[0]
    groups = [matrix[g * 8 : g * 8 + 8, :] for g in range(size // 8)]
    lane = lax.broadcasted_iota(jnp.int32, (8, size), 1)
    line = lax.broadcasted_iota(jnp.int32, (8, size), 0)
    for j in range(size):
        g, r = j // 8, j % 8
        row = groups[g][r : r + 1, :]
        inverse = 1.0 / jnp.broadcast_to(row[:, j : j + 1], (8, size))
        here = lane == j
        scaled = jnp.where(here, inverse, jnp.broadcast_to(row, (8, size)) * inverse)
        for h in range(g, size // 8):
            column = jnp.broadcast_to(groups[h][:, j : j + 1], (8, size))
            new = jnp.where(here, 0.0, groups[h]) - column * scaled
            groups[h] = jnp.where(line > r, new, groups[h]) if h == g else new
    out = []
    for h in range(size // 8):
        diagonal = lane == line + h * 8
        pivot = jnp.sum(jnp.where(diagonal, groups[h], 0.0), axis=1, keepdims=True)
        root = 1.0 / jnp.sqrt(pivot)
        body = jnp.where(lane < line + h * 8, groups[h], jnp.where(diagonal, 1.0, 0.0))
        out.append(body * root)
    return jnp.concatenate(out, axis=0)


def factor_kernel(full_ref, merged_ref, basis_ref, coef_ref):
    ff, rank = full_ref.shape
    half = rank // 2
    sketched = full_ref[...]
    turned = sketched.T
    gram = exact_dot(turned, sketched, ((1,), (0,))) / ff
    first = inverse_factor(gram[:half, :half])
    lower = exact_dot(gram[half:, :half], first, ((1,), (1,)))
    second = inverse_factor(gram[half:, half:] - exact_dot(lower, lower, ((1,), (1,))))
    corner = -exact_dot(second, exact_dot(lower, first, ((1,), (0,))), ((1,), (0,)))
    inverse = jnp.concatenate(
        [
            jnp.concatenate([first, jnp.zeros((half, half), jnp.float32)], axis=1),
            jnp.concatenate([corner, second], axis=1),
        ],
        axis=0,
    )
    turned_orth = exact_dot(inverse, turned, ((1,), (0,))).astype(jnp.bfloat16)
    coef_ref[...] = jnp.dot(
        turned_orth, merged_ref[...], preferred_element_type=jnp.float32
    ) * (1.0 / math.sqrt(ff))
    count = basis_ref.shape[0]
    place = lax.rem(lax.axis_index("expert"), GROUP) * 2 + lax.axis_index("shard")
    mine = full_ref[pl.ds(pl.multiple_of(place * count, count), count), :]
    basis_ref[...] = exact_dot(mine, inverse, ((1,), (1,)))


def factor(full, merged):
    ff, rank = full.shape
    vmem = pl.BlockSpec(memory_space=pltpu.VMEM)
    return pl.pallas_call(
        factor_kernel,
        out_shape=(
            jax.ShapeDtypeStruct((ff // (2 * GROUP), rank), jnp.float32),
            jax.ShapeDtypeStruct((rank, merged.shape[1]), jnp.float32),
        ),
        in_specs=[vmem, vmem],
        out_specs=(vmem, vmem),
        compiler_params=pltpu.CompilerParams(vmem_limit_bytes=LIMIT),
        name="factor",
    )(full, merged)


def mixing_pairs(clusters, frequency):
    count = clusters.shape[0]
    position = lax.axis_index("expert")
    own = position // GROUP
    freq = frequency.astype(jnp.float32)
    same = clusters[:, None] == clusters[None, :]
    totals = jnp.sum(jnp.where(same, freq[None, :], 0.0), axis=1)
    weight = (freq / totals).astype(jnp.bfloat16).astype(jnp.float32)
    sources = own * GROUP + ((position % GROUP) ^ jnp.arange(GROUP, dtype=jnp.int32))
    chosen = sources[:, None] == jnp.arange(count, dtype=jnp.int32)[None, :]
    wanted = jnp.stack([own, own ^ 1])
    picked = chosen[None, :, :] & (clusters[None, None, :] == wanted[:, None, None])
    return jnp.sum(jnp.where(picked, weight[None, None, :], 0.0), axis=2)


def on_device(expert_rows, sketch, permutation, clusters, frequency):
    mix = mixing_pairs(clusters, frequency)
    merged, full = merge(mix, permutation, expert_rows[0], sketch)
    basis, coef = factor(full, merged)
    return merged[None], basis[None], coef[None]


def solution(mesh):
    return jax.shard_map(
        on_device,
        mesh=mesh,
        in_specs=(P("expert", None, "shard"), P("shard", None), P("expert", None), P(), P()),
        out_specs=(
            P("expert", None, "shard"),
            P("expert", "shard", None),
            P("expert", None, "shard"),
        ),
        check_vma=False,
    )
```

time: 481 us -> 179 us (0.37)
  waiting for transfers between devices: 278 us -> 0 us
  Pallas kernels: 0 us -> 173 us
  other arithmetic: 64.4 us -> 3.77 us
  local copies, waits for them, and re-layouts: 52 us -> 1.28 us
  starting transfers between devices: 48.7 us -> 0 us
  matrix products: 22.1 us -> 0 us
  between operations: 15.5 us -> 0.68 us
    all_to_all x2 -> x0, waiting for transfers between devices: 188 us -> none  [the longest x1 148 us: on_device(): lax.all_to_all(permuted.reshape(experts, piece_rows, part_cols), 'expert'...]
    pallas_call x0 -> x2, Pallas kernels: none -> 173 us  [the longest x1 129 us: merge(): pl.pallas_call(merge_kernel, out_shape=(jax.ShapeDtypeStruct((ff, width),...]
    ppermute x2 -> x0, waiting for transfers between devices: 64.9 us -> none  [from_partner(): lax.ppermute(value, axis, [(i, i ^ 1 << distance) for i in range(lax.axis...]
    another operation x9 -> x1, other arithmetic: 60.6 us -> 0.07 us  [mixing_pairs(): wanted = jnp.stack([own, own ^ 1])]
    all_to_all x2 -> x0, starting transfers between devices: 44.1 us -> none  [the longest x1 35.6 us: on_device(): lax.all_to_all(merged_relay.reshape(experts, piece_rows, block_cols), 'ex...]
    psum x1 -> x0, waiting for transfers between devices: 24.7 us -> none  [on_device(): sketched = lax.psum(partial_sketch, 'shard')]
    gather x1 -> x0, local copies, waits for them, and re-layouts: 19.3 us -> none  [on_device(): permuted = local_rows[inverse]]
    dot_general x4 -> x0, matrix products: 14.9 us -> none  [the longest x1 7.96 us: on_device(): jnp.einsum('ce,etgw->cgtw', mixing, spread, preferred_element_type=jnp.fl...]
  transfers between devices with their start and end apart: 5 -> 0, of which waited for: 5 -> 0; matrix products, arithmetic and copies ran while one was open for 0% -> 0% of each run, Pallas kernels for 0% -> 0%
where the time goes in v1:
time: 179 us; the launch traced here: 178 us
  Pallas kernels  173 us (97%)
  other arithmetic  3.77 us (2%)
    pallas_call x1, Pallas kernels, merge(): pl.pallas_call(merge_kernel, out_shape=(jax.ShapeDtypeStruct((ff, width),...  129 us
    pallas_call x1, Pallas kernels, factor(): pl.pallas_call(factor_kernel, out_shape=(jax.ShapeDtypeStruct((ff // (2 *...  43.8 us

profile of v1, /device:TPU:0, one launch (start us, length us, event | category | flops | bytes accessed | tf_op | source)
XLA Modules:
  0.0 178.3 jit_solution(5932846884724956680)
XLA Ops:
  0.7 0.1 iota_compare_fusion
  0.7 0.1 pad_add_fusion
  0.8 0.7 broadcast_compare_fusion
  1.5 0.7 convert_element_type.9
  2.2 0.9 select_reduce_fusion
  3.1 0.7 convert_convert_fusion
  3.8 0.7 select_reduce_fusion.1.mix_ref
  4.4 128.7 %merge.1 = (bf16[1536,640]{1,0:T(8,128)(2,1)}, f32[1536,256]{1,0:T(8,128)}) custom-call(f32[2,4]{1,0:T(2,128)} %select_reduce_fusion.1.mix_ref, s32[1,1536]{1,0:T(1,128)} %perm_ref.1, bf16[1536,2560]{1,0:T(8,128)(2,1)} %bitcast.6, bf16[2560,256]{1,0:T(8,128)(2,1)} %sketch_ref.1), custom_call_target="tpu_custom_call" | custom-call | tf_op jit(solution)/shard_map/merge/pallas_call | solution.py:258
  133.2 0.0 copy-start
  133.2 43.8 %factor.1 = (f32[192,256]{1,0:T(8,128)}, f32[256,640]{1,0:T(8,128)}) custom-call(f32[1536,256]{1,0:T(8,128)} %get-tuple-element.8.full_ref, bf16[1536,640]{1,0:T(8,128)(2,1)} %get-tuple-element.7.merged_ref), custom_call_target="tpu_custom_call" | custom-call | tf_op jit(solution)/shard_map/factor/pallas_call | solution.py:374
  177.0 0.0 copy-done
  177.0 1.3 copy.9
  (1 shorter events, 0.0 us)
Async XLA Ops:
  133.2 43.8 %copy-start = (bf16[1536,640]{1,0:T(8,128)(2,1)S(1)}, bf16[1536,640]{1,0:T(8,128)(2,1)}, u32[]{:S(2)}) copy-start(bf16[1536,640]{1,0:T(8,128)(2,1)} %get-tuple-element.7.merged_ref) | copy-start | bytes 5898244

commit v2 on v1

--- a/solution.py
+++ b/solution.py
@@ -22,7 +22,8 @@
 
 
 def merge_kernel(
-    mix_ref,
+    clusters_ref,
+    frequency_ref,
     perm_ref,
     rows_ref,
     sketch_ref,
@@ -32,6 +33,8 @@
     onehot,
     blocks,
     kept,
+    wide_send,
+    wide_recv,
     zsend,
     zrecv,
     sk,
@@ -66,8 +69,8 @@
     ff, width = merged_ref.shape
     tile = ff // GROUP
     half = tile // 2
-    rank = full_ref.shape[1]
     chunks = column_chunks(width)
+    lanes = chunks[0][1]
     peer_slot = {
         0: slot,
         1: slot + 1 - 2 * lax.rem(slot, 2),
@@ -134,14 +137,42 @@
     for d in (1, 2, 3):
         perm_copies[d].wait()
         build(d, peer_perm[d - 1])
+    window = position - lax.rem(position, 2 * GROUP)
+    own = lax.div(position, GROUP)
+    other = own + 1 - 2 * lax.rem(own, 2)
+
+    def shares(cluster):
+        total = jnp.int32(0)
+        for e in range(2 * GROUP):
+            member = clusters_ref[window + e] == cluster
+            total = total + jnp.where(member, frequency_ref[window + e], 0)
+        total = jnp.full((1, lanes), total).astype(jnp.float32)
+        rows = []
+        for d in range(GROUP):
+            e = plane + peer_slot[d]
+            part_of = jnp.where(clusters_ref[e] == cluster, frequency_ref[e], 0)
+            weight = jnp.full((1, lanes), part_of).astype(jnp.float32) / total
+            rows.append(weight.astype(jnp.bfloat16).astype(jnp.float32))
+        return rows
+
+    keep_share, give_share = shares(own), shares(other)
     own_copy.wait()
     sk_copy.wait()
 
+    def tile_of(i):
+        low = lax.rem(slot + 3 - i, 2)
+        high = lax.rem(lax.div(slot, 2) + lax.div(3 - i, 2), 2)
+        return high * 2 + low
+
     def z_copy(c, t):
         start, step = chunks[c]
-        first = pl.multiple_of(t * tile, tile)
-        view = (pl.ds(first, tile), pl.ds(start, step))
-        return remote(zsend.at[view], zrecv.at[view], z_send.at[c, t], z_recv.at[c, t], across)
+        rows = pl.ds(pl.multiple_of(t * tile, tile), tile)
+        if c == 0:
+            source, target = wide_send.at[rows, :], wide_recv.at[rows, :]
+        else:
+            view = (rows, pl.ds(start - lanes, step))
+            source, target = zsend.at[view], zrecv.at[view]
+        return remote(source, target, z_send.at[c, t], z_recv.at[c, t], across)
 
     def compute(c):
         start, step = chunks[c]
@@ -149,29 +180,36 @@
             row_copies[c, d].wait()
 
         @pl.loop(0, GROUP)
-        def _(t):
-            first = pl.multiple_of(t * tile, tile)
+        def _(i):
+            t = tile_of(i)
+            rows = pl.ds(pl.multiple_of(t * tile, tile), tile)
             keep = jnp.zeros((tile, step), jnp.float32)
             give = jnp.zeros((tile, step), jnp.float32)
-            for d in range(4):
+            for d in range(GROUP):
                 moved = jnp.dot(
-                    onehot[d, pl.ds(first, tile), :],
+                    onehot[d, rows, :],
                     blocks[d, :, start : start + step],
                     preferred_element_type=jnp.float32,
                 )
-                keep = keep + mix_ref[0, d] * moved
-                give = give + mix_ref[1, d] * moved
-            kept[pl.ds(first, tile), start : start + step] = keep
-            zsend[pl.ds(first, tile), start : start + step] = give.astype(jnp.bfloat16)
+                keep = keep + keep_share[d][:, :step] * moved
+                give = give + give_share[d][:, :step] * moved
+            kept[rows, start : start + step] = keep
+            if c == 0:
+                wide_send[rows, :] = give
+            else:
+                zsend[rows, start - lanes : start - lanes + step] = give.astype(jnp.bfloat16)
             z_copy(c, t).start()
 
     def finalize(c, t):
         start, step = chunks[c]
-        first = pl.multiple_of(t * tile, tile)
+        rows = pl.ds(pl.multiple_of(t * tile, tile), tile)
         z_copy(c, t).wait()
-        merged_ref[pl.ds(first, tile), start : start + step] = (
-            kept[pl.ds(first, tile), start : start + step]
-            + zrecv[pl.ds(first, tile), start : start + step].astype(jnp.float32)
+        if c == 0:
+            came = wide_recv[rows, :]
+        else:
+            came = zrecv[rows, start - lanes : start - lanes + step].astype(jnp.float32)
+        merged_ref[rows, start : start + step] = (
+            kept[rows, start : start + step] + came
         ).astype(jnp.bfloat16)
 
     last = len(chunks) - 1
@@ -180,8 +218,8 @@
         if c >= 1:
 
             @pl.loop(0, GROUP)
-            def _(t):
-                finalize(c - 1, t)
+            def _(i):
+                finalize(c - 1, tile_of(i))
 
     def core_copy(t):
         first = pl.multiple_of(t * tile + other_core * half, half)
@@ -193,33 +231,30 @@
             beside,
         )
 
-    @pl.loop(0, GROUP)
-    def _(t):
-        finalize(last, t)
-        first = pl.multiple_of(t * tile, tile)
-        part[pl.ds(first, tile), :] = jnp.dot(
-            merged_ref[pl.ds(first, tile), :], sk[...], preferred_element_type=jnp.float32
-        )
-        core_copy(t).start()
-
-    @pl.loop(0, GROUP)
-    def _(t):
+    rs_copies = {}
+
+    def gather_tile(d):
+        t = peer_slot[d]
         core_copy(t).wait()
         first = pl.multiple_of(t * tile + core * half, half)
         summed[t] = part[pl.ds(first, half), :] + core_rx[t]
-
-    rs_copies = {}
-    for d in (3, 1, 2):
-        rs_copies[d] = remote(
-            summed.at[peer_slot[d]],
-            group_rx.at[d - 1],
-            rs_send.at[d - 1],
-            rs_recv.at[d - 1],
-            peer[d],
-        )
-        rs_copies[d].start()
+        if d:
+            rs_copies[d] = remote(
+                summed.at[t], group_rx.at[d - 1], rs_send.at[d - 1], rs_recv.at[d - 1], peer[d]
+            )
+            rs_copies[d].start()
+
+    for d in (3, 2, 1, 0):
+        t = peer_slot[d]
+        finalize(last, t)
+        rows = pl.ds(pl.multiple_of(t * tile, tile), tile)
+        part[rows, :] = jnp.dot(merged_ref[rows, :], sk[...], preferred_element_type=jnp.float32)
+        core_copy(t).start()
+        if d < 3:
+            gather_tile(d + 1)
+    gather_tile(0)
     total = summed[slot]
-    for d in (1, 2, 3):
+    for d in (3, 2, 1):
         rs_copies[d].wait()
         total = total + group_rx[d - 1]
     mine[...] = total
@@ -246,11 +281,12 @@
         full_ref[b * half : (b + 1) * half, :] = gathered[b]
 
 
-def merge(mix, perm, rows, sketch):
+def merge(clusters, frequency, perm, rows, sketch):
     ff, part_cols = rows.shape
     width = part_cols // GROUP
     rank = sketch.shape[1]
     half = ff // (2 * GROUP)
+    lanes = column_chunks(width)[0][1]
     chunks = len(column_chunks(width))
     dma = pltpu.SemaphoreType.DMA
     vmem = pl.BlockSpec(memory_space=pltpu.VMEM)
@@ -263,6 +299,7 @@
         ),
         in_specs=[
             pl.BlockSpec(memory_space=pltpu.SMEM),
+            pl.BlockSpec(memory_space=pltpu.SMEM),
             vmem,
             pl.BlockSpec(memory_space=pl.ANY),
             pl.BlockSpec(memory_space=pl.ANY),
@@ -273,8 +310,10 @@
             pltpu.VMEM((4, ff, ff), bf16),
             pltpu.VMEM((4, ff, width), bf16),
             pltpu.VMEM((ff, width), f32),
-            pltpu.VMEM((ff, width), bf16),
-            pltpu.VMEM((ff, width), bf16),
+            pltpu.VMEM((ff, lanes), f32),
+            pltpu.VMEM((ff, lanes), f32),
+            pltpu.VMEM((ff, width - lanes), bf16),
+            pltpu.VMEM((ff, width - lanes), bf16),
             pltpu.VMEM((width, rank), bf16),
             pltpu.VMEM((ff, rank), f32),
             pltpu.VMEM((GROUP, half, rank), f32),
@@ -303,7 +342,7 @@
             collective_id=0, has_side_effects=True, vmem_limit_bytes=LIMIT
         ),
         name="merge",
-    )(mix, perm, rows, sketch)
+    )(clusters, frequency, perm, rows, sketch)
 
 
 def exact_dot(left, right, dims):
@@ -316,32 +355,64 @@
     )
 
 
+def spread(value, row, column):
+    size = value.shape[1]
+    line = jnp.broadcast_to(value[row : row + 1, :], (8, size))
+    return jnp.broadcast_to(line[:, column : column + 1], (8, size))
+
+
 def inverse_factor(matrix):
     size = matrix.shape[0]
-    groups = [matrix[g * 8 : g * 8 + 8, :] for g in range(size // 8)]
+    count = size // 8
+    groups = [matrix[g * 8 : g * 8 + 8, :] for g in range(count)]
     lane = lax.broadcasted_iota(jnp.int32, (8, size), 1)
     line = lax.broadcasted_iota(jnp.int32, (8, size), 0)
-    for j in range(size):
-        g, r = j // 8, j % 8
-        row = groups[g][r : r + 1, :]
-        inverse = 1.0 / jnp.broadcast_to(row[:, j : j + 1], (8, size))
-        here = lane == j
-        scaled = jnp.where(here, inverse, jnp.broadcast_to(row, (8, size)) * inverse)
-        for h in range(g, size // 8):
-            column = jnp.broadcast_to(groups[h][:, j : j + 1], (8, size))
-            new = jnp.where(here, 0.0, groups[h]) - column * scaled
-            groups[h] = jnp.where(line > r, new, groups[h]) if h == g else new
     out = []
-    for h in range(size // 8):
-        diagonal = lane == line + h * 8
-        pivot = jnp.sum(jnp.where(diagonal, groups[h], 0.0), axis=1, keepdims=True)
-        root = 1.0 / jnp.sqrt(pivot)
-        body = jnp.where(lane < line + h * 8, groups[h], jnp.where(diagonal, 1.0, 0.0))
-        out.append(body * root)
+    for g in range(count):
+        base = g * 8
+        inside = (lane >= base) & (lane < base + 8)
+        pivot = [[spread(groups[g], r, base + s) for s in range(r + 1)] for r in range(8)]
+        seeded = jnp.where(inside, jnp.where(lane == line + base, 1.0, 0.0), groups[g])
+        rows = [jnp.broadcast_to(seeded[r : r + 1, :], (8, size)) for r in range(8)]
+        inverses, factors = [], {}
+        for s in range(8):
+            inverse = 1.0 / pivot[s][s]
+            inverses.append(inverse)
+            for r in range(s + 1, 8):
+                factors[r, s] = pivot[r][s] * inverse
+            for r in range(s + 1, 8):
+                for t in range(s + 1, r + 1):
+                    pivot[r][t] = pivot[r][t] - factors[r, s] * pivot[t][s]
+                rows[r] = rows[r] - factors[r, s] * rows[s]
+        block = rows[7] * lax.rsqrt(pivot[7][7])
+        for r in range(7):
+            block = jnp.where(line == r, rows[r] * lax.rsqrt(pivot[r][r]), block)
+        out.append(jnp.where(lane <= line + base, block, 0.0))
+        if g == count - 1:
+            break
+        back = [None] * 8
+        for s in reversed(range(8)):
+            value = rows[s] * inverses[s]
+            for r in reversed(range(s + 1, 8)):
+                value = value - factors[r, s] * back[r]
+            back[s] = value
+        for h in range(g + 1, count):
+            columns = [
+                jnp.broadcast_to(groups[h][:, base + s : base + s + 1], (8, size))
+                for s in range(8)
+            ]
+            value = jnp.where(inside, 0.0, groups[h])
+            terms = [columns[s] * back[s] for s in range(8)]
+            groups[h] = value - (
+                ((terms[0] + terms[1]) + (terms[2] + terms[3]))
+                + ((terms[4] + terms[5]) + (terms[6] + terms[7]))
+            )
     return jnp.concatenate(out, axis=0)
 
 
-def factor_kernel(full_ref, merged_ref, basis_ref, coef_ref):
+def factor_kernel(full_ref, merged_ref, out_ref, basis_ref, coef_ref, out_sem):
+    out_copy = pltpu.make_async_copy(merged_ref, out_ref, out_sem)
+    out_copy.start()
     ff, rank = full_ref.shape
     half = rank // 2
     sketched = full_ref[...]
@@ -366,6 +437,7 @@
     place = lax.rem(lax.axis_index("expert"), GROUP) * 2 + lax.axis_index("shard")
     mine = full_ref[pl.ds(pl.multiple_of(place * count, count), count), :]
     basis_ref[...] = exact_dot(mine, inverse, ((1,), (1,)))
+    out_copy.wait()
 
 
 def factor(full, merged):
@@ -374,35 +446,21 @@
     return pl.pallas_call(
         factor_kernel,
         out_shape=(
+            jax.ShapeDtypeStruct(merged.shape, merged.dtype),
             jax.ShapeDtypeStruct((ff // (2 * GROUP), rank), jnp.float32),
             jax.ShapeDtypeStruct((rank, merged.shape[1]), jnp.float32),
         ),
         in_specs=[vmem, vmem],
-        out_specs=(vmem, vmem),
+        out_specs=(pl.BlockSpec(memory_space=pl.ANY), vmem, vmem),
+        scratch_shapes=[pltpu.SemaphoreType.DMA],
         compiler_params=pltpu.CompilerParams(vmem_limit_bytes=LIMIT),
         name="factor",
     )(full, merged)
 
 
-def mixing_pairs(clusters, frequency):
-    count = clusters.shape[0]
-    position = lax.axis_index("expert")
-    own = position // GROUP
-    freq = frequency.astype(jnp.float32)
-    same = clusters[:, None] == clusters[None, :]
-    totals = jnp.sum(jnp.where(same, freq[None, :], 0.0), axis=1)
-    weight = (freq / totals).astype(jnp.bfloat16).astype(jnp.float32)
-    sources = own * GROUP + ((position % GROUP) ^ jnp.arange(GROUP, dtype=jnp.int32))
-    chosen = sources[:, None] == jnp.arange(count, dtype=jnp.int32)[None, :]
-    wanted = jnp.stack([own, own ^ 1])
-    picked = chosen[None, :, :] & (clusters[None, None, :] == wanted[:, None, None])
-    return jnp.sum(jnp.where(picked, weight[None, None, :], 0.0), axis=2)
-
-
 def on_device(expert_rows, sketch, permutation, clusters, frequency):
-    mix = mixing_pairs(clusters, frequency)
-    merged, full = merge(mix, permutation, expert_rows[0], sketch)
-    basis, coef = factor(full, merged)
+    merged, full = merge(clusters, frequency, permutation, expert_rows[0], sketch)
+    merged, basis, coef = factor(full, merged)
     return merged[None], basis[None], coef[None]
 
 

time: 179 us -> 146 us (0.82)
  Pallas kernels: 173 us -> 145 us
  other arithmetic: 3.77 us -> 0 us
    pallas_call x1, Pallas kernels: 43.8 us -> 19.6 us  [factor(): pl.pallas_call(factor_kernel, out_shape=(jax.ShapeDtypeStruct(merged.shap...]
    pallas_call x1, Pallas kernels: 129 us -> 126 us  [merge(): pl.pallas_call(merge_kernel, out_shape=(jax.ShapeDtypeStruct((ff, width),...]
where the time goes in v2:
time: 146 us
  Pallas kernels  145 us (99%)
    pallas_call x1, Pallas kernels, merge(): pl.pallas_call(merge_kernel, out_shape=(jax.ShapeDtypeStruct((ff, width),...  126 us
    pallas_call x1, Pallas kernels, factor(): pl.pallas_call(factor_kernel, out_shape=(jax.ShapeDtypeStruct(merged.shap...  19.6 us

profile of v2, /device:TPU:0, one launch (start us, length us, event | category | flops | bytes accessed | tf_op | source)
XLA Modules:
  0.0 145.9 jit_solution(17028162708269413146)
XLA Ops:
  0.6 125.5 %merge.1 = (bf16[1536,640]{1,0:T(8,128)(2,1)}, f32[1536,256]{1,0:T(8,128)}) custom-call(s32[16]{0:T(128)} %clusters_ref.1, s32[16]{0:T(128)} %frequency_ref.1, s32[1,1536]{1,0:T(1,128)} %perm_ref.1, bf16[1536,2560]{1,0:T(8,128)(2,1)} %bitcast.4, bf16[2560,256]{1,0:T(8,128)(2,1)} %sketch_ref.1), custom_call_target="tpu_custom_call" | custom-call | tf_op jit(solution)/shard_map/merge/pallas_call | solution.py:294
  126.1 19.6 %factor.1 = (bf16[1536,640]{1,0:T(8,128)(2,1)}, f32[192,256]{1,0:T(8,128)}, f32[256,640]{1,0:T(8,128)}) custom-call(f32[1536,256]{1,0:T(8,128)} %get-tuple-element.8.full_ref, bf16[1536,640]{1,0:T(8,128)(2,1)} %get-tuple-element.9.merged_ref), custom_call_target="tpu_custom_call" | custom-call | tf_op jit(solution)/shard_map/factor/pallas_call | solution.py:446

commit v3 on v2

--- a/solution.py
+++ b/solution.py
@@ -29,6 +29,7 @@
     sketch_ref,
     merged_ref,
     full_ref,
+    total_ref,
     peer_perm,
     onehot,
     blocks,
@@ -257,7 +258,9 @@
     for d in (3, 2, 1):
         rs_copies[d].wait()
         total = total + group_rx[d - 1]
-    mine[...] = total
+    total_ref[...] = total
+    rounded = total.astype(jnp.bfloat16)
+    mine[...] = rounded
     place = slot * 2 + core
     ag_copies = {}
     for d in (3, 1, 2):
@@ -267,7 +270,7 @@
         ag_copies[d].start()
     forwards = [remote(mine, gathered.at[place], fw_send.at[0], fw_recv.at[0], beside)]
     forwards[0].start()
-    gathered[place] = total
+    gathered[place] = rounded
     for d in (1, 2, 3):
         ag_copies[d].wait()
         came = peer_slot[d] * 2 + core
@@ -295,7 +298,8 @@
         merge_kernel,
         out_shape=(
             jax.ShapeDtypeStruct((ff, width), bf16),
-            jax.ShapeDtypeStruct((ff, rank), f32),
+            jax.ShapeDtypeStruct((ff, rank), bf16),
+            jax.ShapeDtypeStruct((half, rank), f32),
         ),
         in_specs=[
             pl.BlockSpec(memory_space=pltpu.SMEM),
@@ -304,7 +308,7 @@
             pl.BlockSpec(memory_space=pl.ANY),
             pl.BlockSpec(memory_space=pl.ANY),
         ],
-        out_specs=(vmem, vmem),
+        out_specs=(vmem, vmem, vmem),
         scratch_shapes=[
             pltpu.VMEM((3, 1, ff), jnp.int32),
             pltpu.VMEM((4, ff, ff), bf16),
@@ -319,8 +323,8 @@
             pltpu.VMEM((GROUP, half, rank), f32),
             pltpu.VMEM((GROUP, half, rank), f32),
             pltpu.VMEM((3, half, rank), f32),
-            pltpu.VMEM((half, rank), f32),
-            pltpu.VMEM((2 * GROUP, half, rank), f32),
+            pltpu.VMEM((half, rank), bf16),
+            pltpu.VMEM((2 * GROUP, half, rank), bf16),
             dma((3,)),
             dma((3,)),
             dma,
@@ -410,14 +414,13 @@
     return jnp.concatenate(out, axis=0)
 
 
-def factor_kernel(full_ref, merged_ref, out_ref, basis_ref, coef_ref, out_sem):
+def factor_kernel(full_ref, total_ref, merged_ref, out_ref, basis_ref, coef_ref, out_sem):
     out_copy = pltpu.make_async_copy(merged_ref, out_ref, out_sem)
     out_copy.start()
     ff, rank = full_ref.shape
     half = rank // 2
-    sketched = full_ref[...]
-    turned = sketched.T
-    gram = exact_dot(turned, sketched, ((1,), (0,))) / ff
+    turned = full_ref[...].astype(jnp.float32).T.astype(jnp.bfloat16)
+    gram = jnp.dot(turned, full_ref[...], preferred_element_type=jnp.float32) / ff
     first = inverse_factor(gram[:half, :half])
     lower = exact_dot(gram[half:, :half], first, ((1,), (1,)))
     second = inverse_factor(gram[half:, half:] - exact_dot(lower, lower, ((1,), (1,))))
@@ -429,38 +432,40 @@
         ],
         axis=0,
     )
-    turned_orth = exact_dot(inverse, turned, ((1,), (0,))).astype(jnp.bfloat16)
+    turned_orth, rest = jnp.zeros((rank, ff), jnp.float32), inverse
+    for _ in range(3):
+        piece = rest.astype(jnp.bfloat16)
+        rest = rest - piece.astype(jnp.float32)
+        turned_orth = turned_orth + jnp.dot(piece, turned, preferred_element_type=jnp.float32)
+    turned_orth = turned_orth.astype(jnp.bfloat16)
     coef_ref[...] = jnp.dot(
         turned_orth, merged_ref[...], preferred_element_type=jnp.float32
     ) * (1.0 / math.sqrt(ff))
-    count = basis_ref.shape[0]
-    place = lax.rem(lax.axis_index("expert"), GROUP) * 2 + lax.axis_index("shard")
-    mine = full_ref[pl.ds(pl.multiple_of(place * count, count), count), :]
-    basis_ref[...] = exact_dot(mine, inverse, ((1,), (1,)))
+    basis_ref[...] = exact_dot(total_ref[...], inverse, ((1,), (1,)))
     out_copy.wait()
 
 
-def factor(full, merged):
+def factor(full, total, merged):
     ff, rank = full.shape
     vmem = pl.BlockSpec(memory_space=pltpu.VMEM)
     return pl.pallas_call(
         factor_kernel,
         out_shape=(
             jax.ShapeDtypeStruct(merged.shape, merged.dtype),
-            jax.ShapeDtypeStruct((ff // (2 * GROUP), rank), jnp.float32),
+            jax.ShapeDtypeStruct(total.shape, jnp.float32),
             jax.ShapeDtypeStruct((rank, merged.shape[1]), jnp.float32),
         ),
-        in_specs=[vmem, vmem],
+        in_specs=[vmem, vmem, vmem],
         out_specs=(pl.BlockSpec(memory_space=pl.ANY), vmem, vmem),
         scratch_shapes=[pltpu.SemaphoreType.DMA],
         compiler_params=pltpu.CompilerParams(vmem_limit_bytes=LIMIT),
         name="factor",
-    )(full, merged)
+    )(full, total, merged)
 
 
 def on_device(expert_rows, sketch, permutation, clusters, frequency):
-    merged, full = merge(clusters, frequency, permutation, expert_rows[0], sketch)
-    merged, basis, coef = factor(full, merged)
+    merged, full, total = merge(clusters, frequency, permutation, expert_rows[0], sketch)
+    merged, basis, coef = factor(full, total, merged)
     return merged[None], basis[None], coef[None]
 
 

time: 146 us -> 138 us (0.945)
  Pallas kernels: 145 us -> 137 us
    pallas_call x1, Pallas kernels: 126 us -> 121 us  [merge(): pl.pallas_call(merge_kernel, out_shape=(jax.ShapeDtypeStruct((ff, width),...]
    pallas_call x1, Pallas kernels: 19.6 us -> 16.1 us  [factor(): pl.pallas_call(factor_kernel, out_shape=(jax.ShapeDtypeStruct(merged.shap...]
where the time goes in v3:
time: 138 us
  Pallas kernels  137 us (99%)
    pallas_call x1, Pallas kernels, merge(): pl.pallas_call(merge_kernel, out_shape=(jax.ShapeDtypeStruct((ff, width),...  121 us
    pallas_call x1, Pallas kernels, factor(): pl.pallas_call(factor_kernel, out_shape=(jax.ShapeDtypeStruct(merged.shap...  16.1 us

profile of v3, /device:TPU:0, one launch (start us, length us, event | category | flops | bytes accessed | tf_op | source)
XLA Modules:
  0.0 137.6 jit_solution(17690793186344951018)
XLA Ops:
  0.6 120.7 %merge.1 = (bf16[1536,640]{1,0:T(8,128)(2,1)}, bf16[1536,256]{1,0:T(8,128)(2,1)}, f32[192,256]{1,0:T(8,128)}) custom-call(s32[16]{0:T(128)} %clusters_ref.1, s32[16]{0:T(128)} %frequency_ref.1, s32[1,1536]{1,0:T(1,128)} %perm_ref.1, bf16[1536,2560]{1,0:T(8,128)(2,1)} %bitcast.4, bf16[2560,256]{1,0:T(8,128)(2,1)} %sketch_ref.1), custom_call_target="tpu_custom_call" | custom-call | tf_op jit(solution)/shard_map/merge/pallas_call | solution.py:297
  121.4 16.1 %factor.1 = (bf16[1536,640]{1,0:T(8,128)(2,1)}, f32[192,256]{1,0:T(8,128)}, f32[256,640]{1,0:T(8,128)}) custom-call(bf16[1536,256]{1,0:T(8,128)(2,1)} %get-tuple-element.9.full_ref, f32[192,256]{1,0:T(8,128)} %get-tuple-element.10.total_ref, bf16[1536,640]{1,0:T(8,128)(2,1)} %get-tuple-element.11.merged_ref), custom_call_target="tpu_custom_call" | custom-call | tf_op jit(solution)/shard_map/factor/pallas_call | solution.py:451
